TPU v7x, 32 devices: a whole 2x2x4 slice. The times are simulated.
32 devices in a mesh: row: 8 (over y, x, core), col: 4 (over z).
Axes of the slice: x: 2, y: 2, z: 4, core: 2. Of those that a mesh axis runs over, the one named last changes fastest.
Arguments:
- panel_tiles: float32 [16384, 1024], P('row', 'col'), may hold values from -48 to 48
- left_u: bfloat16 [16384, 6144], P('row', 'col'), may hold values from -8 to 8
- earlier_right_factors: bfloat16 [16384, 6144], P('row', 'col'), may hold values from -0.25 to 0.25
- tile_global_index: int32 [16], replicated, may hold values from 0 to 15, as said below
Outputs:
- panel_factor: float32 [16384, 1024], P('row', 'col')
Inputs may be any that keep to these rules, and one draw needn't show every extreme that they name: `tile_global_index`: A permutation; slot pivot, the one numbered 0, holds the diagonal tile.
All inputs are finite; a program needn't handle non-finite values.
Results may differ from a plain program's by a relative error of at most 0.00053.
Values may be sent and summed in bfloat16 or wider, within the bound.
A program may use at most 128 MiB of HBM per device.

v0:
```python
import jax
import jax.numpy as jnp
from jax import lax
from jax.sharding import PartitionSpec as P

TILE = 1024
RANK = 256
TILE_DEV = 2
COL_DEV = 6


def from_root(value, axis, source):
    kept = jnp.where(lax.axis_index(axis) == source, value, 0).astype(value.dtype)
    return lax.psum(kept, axis)


def local(panel_tiles, left_u, earlier_right_factors, tile_global_index):
    tile_count = tile_global_index.shape[0]
    pivot_position = jnp.sum(
        jnp.where(tile_global_index == 0, jnp.arange(tile_count, dtype=jnp.int32), 0)
    )
    owner_row = pivot_position // TILE_DEV
    local_slot = pivot_position % TILE_DEV
    my_row = lax.axis_index("row")
    my_col = lax.axis_index("col")
    col_width = panel_tiles.shape[1]
    pivot_left = lax.dynamic_slice_in_dim(left_u, local_slot * TILE, TILE, 0)
    pivot_right = lax.dynamic_slice_in_dim(earlier_right_factors, local_slot * TILE, TILE, 0)
    pivot_left, pivot_right = (
        from_root(pivot_left, "row", owner_row),
        from_root(pivot_right, "row", owner_row),
    )
    left_blocks = left_u.reshape(TILE_DEV, TILE, COL_DEV, RANK)
    right_blocks = earlier_right_factors.reshape(TILE_DEV, TILE, COL_DEV, RANK)
    pivot_triple = pivot_right.reshape(TILE, COL_DEV, RANK)
    inner_small = jnp.einsum(
        "tbjr,bjs->tjrs", right_blocks, pivot_triple, preferred_element_type=jnp.float32
    ).astype(jnp.bfloat16)
    left_small = jnp.einsum(
        "tbjr,tjrs->tbjs", left_blocks, inner_small, preferred_element_type=jnp.float32
    ).astype(jnp.bfloat16)
    update_terms = jnp.einsum(
        "nk,mk->nm",
        left_small.reshape(TILE_DEV * TILE, COL_DEV * RANK),
        pivot_left,
        preferred_element_type=jnp.float32,
    )
    placed = lax.dynamic_update_slice_in_dim(
        jnp.zeros_like(update_terms), panel_tiles, my_col * col_width, 1
    )
    updated_tiles = lax.psum(placed - update_terms, "col")
    diagonal = lax.dynamic_slice_in_dim(updated_tiles, local_slot * TILE, TILE, 0)
    identity = jnp.eye(TILE, dtype=jnp.float32)
    cholesky_factor = jnp.linalg.cholesky(diagonal)
    inverted_factor = lax.linalg.triangular_solve(
        cholesky_factor, identity, left_side=True, lower=True
    )
    rows_inv = lax.dynamic_slice_in_dim(inverted_factor, my_col * col_width, col_width, 0)
    rows_inv = from_root(rows_inv, "row", owner_row)
    solved_rows = lax.dot_general(
        updated_tiles,
        rows_inv,
        (((1,), (1,)), ((), ())),
        precision=lax.Precision.HIGHEST,
        preferred_element_type=jnp.float32,
    )
    factor_cols = lax.dynamic_slice_in_dim(cholesky_factor, my_col * col_width, col_width, 1)
    row_tiles = jnp.arange(TILE_DEV * TILE, dtype=jnp.int32) // TILE
    chosen_rows = jnp.logical_and(my_row == owner_row, row_tiles == local_slot)
    return jnp.where(chosen_rows[:, None], jnp.tile(factor_cols, (TILE_DEV, 1)), solved_rows)


def solution(mesh):
    in_specs = (P("row", "col"), P("row", "col"), P("row", "col"), P())
    out_specs = P("row", "col")
    return jax.shard_map(local, mesh=mesh, in_specs=in_specs, out_specs=out_specs, check_vma=False)
```

profile of v0, /device:TPU:0, one launch (start us, length us, event | category | flops | bytes accessed | tf_op | source)
XLA Modules:
  0.0 900.8 jit_solution(1738015696041004447)
XLA Ops:
  10.7 5.9 constant_dynamic-slice_fusion.3
  16.6 3.2 copy.24
  19.8 4.7 copy.25
  24.5 2.0 broadcast_select_fusion.1
  27.5 2.0 broadcast_select_fusion
  29.6 13.5 %reshape.127 = bf16[2,1024,6,256]{3,2,1,0:T(8,128)(2,1)} reshape(bf16[2048,1536]{1,0:T(8,128)(2,1)} %param.5) | data formatting | bytes 12582912 | tf_op jit(solution)/shard_map/reshape | solution.py:33
  43.1 13.4 %reshape.126 = bf16[2,1024,6,256]{3,2,1,0:T(8,128)(2,1)} reshape(bf16[2048,1536]{1,0:T(8,128)(2,1)} %param.6) | data formatting | bytes 12582912 | tf_op jit(solution)/shard_map/reshape | solution.py:34
  56.5 1.9 copy.9
  58.5 4.3 broadcast_in_dim.26
  64.3 72.1 %all-reduce.10.cloned.1.call-done = (bf16[1024,6,256]{0,2,1:T(8,128)(2,1)}, bf16[1024,1536]{0,1:T(8,128)(2,1)}) async-done(((bf16[1024,6,256]{0,2,1:T(8,128)(2,1)}, bf16[1024,1536]{0,1:T(8,128)(2,1)}), (bf16[1024,6,256]{0,2,1:T(8,128)(2,1)}, bf16[1024,1536]{0,1:T(8,128)(2,1)})) %all-reduce.10.cloned.1.call-update) | async-done | bytes 6291472 | tf_op jit(solution)/shard_map/psum | solution.py:14
  136.3 16.6 %convert_bitcast_fusion = bf16[2,1024,6,256]{1,3,2,0:T(8,128)(2,1)} fusion(bf16[2,1024,6,256]{3,2,1,0:T(8,128)(2,1)} %reshape.127, bf16[2,1024,6,256]{3,2,1,0:T(8,128)(2,1)} %reshape.126, bf16[1024,6,256]{0,2,1:T(8,128)(2,1)} %get-tuple-element.21), kind=kOutput, calls=%fused_computation.6 | convolution fusion | flops 3225157632 | bytes 22020096 | tf_op jit(solution)/shard_map/tbjr,tjrs->tbjs/dot_general | solution.py:39
  152.9 11.9 %copy.14 = bf16[2,1024,6,256]{1,0,3,2:T(2,128)(2,1)S(1)} copy(bf16[2,1024,6,256]{1,3,2,0:T(8,128)(2,1)} %convert_bitcast_fusion) | data formatting | bytes 12582912 | tf_op jit(solution)/shard_map/convert_element_type | solution.py:41
  164.9 2.7 copy.26
  167.5 11.9 %convolution_subtract_fusion = f32[2048,1024]{0,1:T(8,128)} fusion(f32[2048,1024]{0,1:T(8,128)} %constant_dynamic-update-slice_fusion.26, bf16[2048,1536]{0,1:T(8,128)(2,1)S(1)} %bitcast.129, bf16[1024,1536]{0,1:T(8,128)(2,1)S(1)} %copy-done.3), kind=kOutput, calls=%fused_computation.13 | convolution fusion | flops 6444548096 | bytes 26214400 | tf_op jit(solution)/shard_map/nk,mk->nm/dot_general | solution.py:42
  179.8 2.4 fusion.43
  182.3 288.3 %all-reduce.6.cloned.1.call-done = f32[2048,1024]{0,1:T(8,128)} async-done(((f32[2048,1024]{0,1:T(8,128)}), f32[2048,1024]{0,1:T(8,128)}) %all-reduce.6.cloned.1.call-update) | async-done | bytes 8388624 | tf_op jit(solution)/shard_map/psum | solution.py:51
  470.5 4.7 constant_dynamic-slice_fusion.2
  475.3 5.4 copy.17
  480.6 4.4 fusion.4
  485.1 2.0 copy-done.2
  487.1 11.7 %cholesky.223 = f32[128,128]{1,0:T(8,128)S(1)} custom-call(f32[128,128]{1,0:T(8,128)S(1)} %cholesky.580), custom_call_target="Cholesky" | custom-call | tf_op jit(solution)/shard_map/jit(cholesky)/cholesky | solution.py:54
  498.8 2.5 cholesky.255
  501.3 9.8 %custom-call.62 = f32[1,128,128]{1,2,0:T(8,128)S(1)} custom-call(f32[1,128,128]{2,1,0:T(8,128)S(1)} %get-tuple-element.73), custom_call_target="InvertDiagBlocksLowerTriangular" | custom-call | tf_op jit(solution)/shard_map/jit(cholesky)/cholesky | solution.py:54
  511.1 2.4 constant_dynamic-update-slice_fusion.25
  513.5 1.5 convolution_subtract_fusion.6
  515.0 11.9 %cholesky.244 = f32[128,128]{1,0:T(8,128)S(1)} custom-call(f32[128,128]{1,0:T(8,128)S(1)} %cholesky.584), custom_call_target="Cholesky" | custom-call | tf_op jit(solution)/shard_map/jit(cholesky)/cholesky | solution.py:54
  527.5 9.8 %custom-call.63 = f32[1,128,128]{1,2,0:T(8,128)S(1)} custom-call(f32[1,128,128]{2,1,0:T(8,128)S(1)} %get-tuple-element.70), custom_call_target="InvertDiagBlocksLowerTriangular" | custom-call | tf_op jit(solution)/shard_map/jit(cholesky)/cholesky | solution.py:54
  538.6 2.1 convolution_subtract_fusion.7
  540.7 11.7 %cholesky.468 = f32[128,128]{1,0:T(8,128)S(1)} custom-call(f32[128,128]{1,0:T(8,128)S(1)} %cholesky.589), custom_call_target="Cholesky" | custom-call | tf_op jit(solution)/shard_map/jit(cholesky)/cholesky | solution.py:54
  553.1 9.8 %custom-call.64 = f32[1,128,128]{1,2,0:T(8,128)S(1)} custom-call(f32[1,128,128]{2,1,0:T(8,128)S(1)} %get-tuple-element.67), custom_call_target="InvertDiagBlocksLowerTriangular" | custom-call | tf_op jit(solution)/shard_map/jit(cholesky)/cholesky | solution.py:54
  564.1 2.3 convolution_subtract_fusion.8
  566.4 11.9 %cholesky.487 = f32[128,128]{1,0:T(8,128)S(1)} custom-call(f32[128,128]{1,0:T(8,128)S(1)} %cholesky.594), custom_call_target="Cholesky" | custom-call | tf_op jit(solution)/shard_map/jit(cholesky)/cholesky | solution.py:54
  579.0 9.8 %custom-call.65 = f32[1,128,128]{1,2,0:T(8,128)S(1)} custom-call(f32[1,128,128]{2,1,0:T(8,128)S(1)} %get-tuple-element.64), custom_call_target="InvertDiagBlocksLowerTriangular" | custom-call | tf_op jit(solution)/shard_map/jit(cholesky)/cholesky | solution.py:54
  589.9 2.3 convolution_subtract_fusion.9
  592.3 11.7 %cholesky.506 = f32[128,128]{1,0:T(8,128)S(1)} custom-call(f32[128,128]{1,0:T(8,128)S(1)} %cholesky.599), custom_call_target="Cholesky" | custom-call | tf_op jit(solution)/shard_map/jit(cholesky)/cholesky | solution.py:54
  604.6 10.2 %custom-call.66 = f32[1,128,128]{1,2,0:T(8,128)S(1)} custom-call(f32[1,128,128]{2,1,0:T(8,128)S(1)} %get-tuple-element.61), custom_call_target="InvertDiagBlocksLowerTriangular" | custom-call | tf_op jit(solution)/shard_map/jit(cholesky)/cholesky | solution.py:54
  615.8 2.3 convolution_subtract_fusion.10
  618.1 11.7 %cholesky.526 = f32[128,128]{1,0:T(8,128)S(1)} custom-call(f32[128,128]{1,0:T(8,128)S(1)} %cholesky.604), custom_call_target="Cholesky" | custom-call | tf_op jit(solution)/shard_map/jit(cholesky)/cholesky | solution.py:54
  630.5 9.8 %custom-call.67 = f32[1,128,128]{1,2,0:T(8,128)S(1)} custom-call(f32[1,128,128]{2,1,0:T(8,128)S(1)} %get-tuple-element.58), custom_call_target="InvertDiagBlocksLowerTriangular" | custom-call | tf_op jit(solution)/shard_map/jit(cholesky)/cholesky | solution.py:54
  641.2 2.0 convolution_subtract_fusion.11
  643.3 11.7 %cholesky.546 = f32[128,128]{1,0:T(8,128)S(1)} custom-call(f32[128,128]{1,0:T(8,128)S(1)} %cholesky.609), custom_call_target="Cholesky" | custom-call | tf_op jit(solution)/shard_map/jit(cholesky)/cholesky | solution.py:54
  655.6 9.8 %custom-call.68 = f32[1,128,128]{1,2,0:T(8,128)S(1)} custom-call(f32[1,128,128]{2,1,0:T(8,128)S(1)} %get-tuple-element.55), custom_call_target="InvertDiagBlocksLowerTriangular" | custom-call | tf_op jit(solution)/shard_map/jit(cholesky)/cholesky | solution.py:54
  666.3 1.8 convolution_subtract_fusion.12
  668.1 11.7 %cholesky.564 = f32[128,128]{1,0:T(8,128)S(1)} custom-call(f32[128,128]{1,0:T(8,128)S(1)} %convolution_subtract_fusion.12), custom_call_target="Cholesky" | custom-call | tf_op jit(solution)/shard_map/jit(cholesky)/cholesky | solution.py:54
  690.5 4.4 fusion.5
  694.9 22.9 %while.1 = (s32[]{:T(128)}, f32[1024,1024]{1,0:T(8,128)}, s32[8,2]{0,1:T(2,128)S(1)}, f32[8,128,128]{2,1,0:T(8,128)S(1)}, s32[]{:T(128)}) while((s32[]{:T(128)}, f32[1024,1024]{1,0:T(8,128)}, s32[8,2]{0,1:T(2,128)S(1)}, f32[8,128,128]{2,1,0:T(8,128)S(1)}, s32[]{:T(128)}) %tuple.58), condition=%wide.while_cond, body=%wide.while_body.sunk | while | flops 2 | bytes 131189 | solution.py:55
  695.6 2.2 bitcast_dynamic-update-slice_fusion.2
  698.4 2.2 bitcast_dynamic-update-slice_fusion.2
  701.3 2.2 bitcast_dynamic-update-slice_fusion.2
  704.2 2.2 bitcast_dynamic-update-slice_fusion.2
  707.1 2.2 bitcast_dynamic-update-slice_fusion.2
  709.9 2.2 bitcast_dynamic-update-slice_fusion.2
  712.8 2.2 bitcast_dynamic-update-slice_fusion.2
  715.7 2.2 bitcast_dynamic-update-slice_fusion.2
  717.8 78.8 %custom-call.69 = f32[8,128,128]{1,2,0:T(8,128)S(1)} custom-call(f32[8,128,128]{2,1,0:T(8,128)S(1)} %get-tuple-element.12), custom_call_target="InvertDiagBlocksLowerTriangular" | custom-call | tf_op jit(solution)/shard_map/triangular_solve | solution.py:55
  797.2 1.9 convolution_subtract_fusion.5
  799.9 1.6 convolution_subtract_fusion.1
  802.3 2.0 fusion.37
  805.1 2.2 fusion.40
  808.0 2.6 convolution_subtract_fusion.3
  811.4 2.8 convolution_subtract_fusion.2
  814.8 3.5 convolution_subtract_fusion.4
  821.4 55.3 %all-reduce.8.cloned.1.call-done = f32[256,1024]{1,0:T(8,128)} async-done(((f32[256,1024]{1,0:T(8,128)}), f32[256,1024]{1,0:T(8,128)}) %all-reduce.8.cloned.1.call-update) | async-done | bytes 1048592 | tf_op jit(solution)/shard_map/psum | solution.py:14
  876.9 17.0 %convolution_select_fusion = f32[2048,256]{1,0:T(8,128)} fusion(f32[2048,256]{1,0:T(8,128)S(1)} %bitcast.127, f32[2048,1024]{0,1:T(8,128)} %all-reduce.6.cloned.1.call-done, f32[256,1024]{1,0:T(8,128)} %all-reduce.8.cloned.1.call-done, pred[2048]{0:T(1024)(128)(4,1)S(1)} %fusion.93), kind=kOutput, calls=%fused_computation.17 | convolution fusion | flops 6442975232 | bytes 13633536 | tf_op jit(solution)/shard_map/dot_general | solution.py:60
  (76 shorter events, 33.4 us)
Async XLA Ops:
  6.5 129.8 %all-reduce.10.cloned.1.call-start = ((), (), s32[]{:S(2)}) async-start(), calls=%async_computation.2 | async-start | bytes 12582912 | tf_op jit(solution)/shard_map/psum | solution.py:14
  24.5 3.0 copy-start.1
  29.5 441.0 %all-reduce.6.cloned.1.call-start = ((), (), s32[]{:S(2)}) async-start(), calls=%async_computation | async-start | bytes 16777216 | tf_op jit(solution)/shard_map/psum | solution.py:51
  164.9 2.7 copy-start.3
  179.4 697.3 %all-reduce.8.cloned.1.call-start = ((), (), s32[]{:S(2)}) async-start(), calls=%async_computation.1 | async-start | bytes 2097152 | tf_op jit(solution)/shard_map/psum | solution.py:14
  485.1 2.0 copy-start.2
  796.7 3.2 copy-start
Sparse Core Ops, SparseCore 0:
  29.6 106.6 all-reduce.9
  179.6 290.9 all-reduce.5
  820.2 56.4 all-reduce.7
where the time goes:
time: 912 us; the launch traced here: 901 us
  waiting for transfers between devices  416 us (46%)
  other arithmetic  270 us (30%)
  local copies, waits for them, and re-layouts  103 us (11%)
  matrix products  90.7 us (10%)
  between operations  21.6 us (2%)
    psum x1, waiting for transfers between devices, local(): updated_tiles = lax.psum(placed - update_terms, 'col')  288 us
    another operation x31, other arithmetic, local(): cholesky_factor = jnp.linalg.cholesky(diagonal)  173 us
    psum x2, waiting for transfers between devices, from_root(): return lax.psum(kept, axis)  127 us
    another operation x3, other arithmetic, local(): lax.linalg.triangular_solve(cholesky_factor, identity, left_side=True, lo...  83.2 us
    another operation x14, matrix products, local(): cholesky_factor = jnp.linalg.cholesky(diagonal)  23.1 us
    another operation x24, local copies, waits for them, and re-layouts  22.7 us
    another operation x15, matrix products, local(): lax.linalg.triangular_solve(cholesky_factor, identity, left_side=True, lo...  22.2 us
  transfers between devices with their start and end apart: 3, of which 3 were waited for; matrix products, arithmetic and copies ran while one was open for 4% of the time, Pallas kernels for 0%

commit v1 on v0

v1 whole, which is shorter than its diff:
```python
import functools

import jax
import jax.numpy as jnp
from jax import lax
from jax.experimental import pallas as pl
from jax.experimental.pallas import tpu as pltpu
from jax.sharding import PartitionSpec as P

TILE = 1024
RANK = 256

BLK = 128
SUB = 8
F32 = jnp.float32
HI = lax.Precision.HIGHEST


def dot(a, b, dims=((1,), (0,))):
    return lax.dot_general(a, b, (dims, ((), ())), precision=HI, preferred_element_type=F32)


def eliminate(block):
    shape = (SUB, BLK)
    groups = [block[g * SUB:(g + 1) * SUB, :] for g in range(BLK // SUB)]
    lane = lax.broadcasted_iota(jnp.int32, shape, 1)
    sub = lax.broadcasted_iota(jnp.int32, shape, 0)
    for g in range(len(groups)):
        base = g * SUB
        rows = groups[g]
        cols = [jnp.broadcast_to(rows[:, base + j:base + j + 1], shape) for j in range(SUB)]
        out = rows
        for s in range(SUB):
            raw = jnp.broadcast_to(rows[s:s + 1, :], shape)
            here = lane == base + s
            mine = sub == s
            out = jnp.where(mine, raw, out)
            inverse = 1.0 / jnp.broadcast_to(cols[s][s:s + 1, :], shape)
            factor = jnp.where(mine, 0.0, cols[s] * inverse)
            unit = jnp.where(here, 1.0, raw)
            kept = jnp.where(here, 0.0, rows)
            rows = jnp.where(mine, unit * inverse, kept - factor * unit)
            for j in range(s + 1, SUB):
                head = jnp.broadcast_to(cols[j][s:s + 1, :], shape)
                cols[j] = jnp.where(mine, head * inverse, cols[j] - factor * head)
        groups[g] = out
        if g + 1 == len(groups):
            break
        reduced = [jnp.broadcast_to(rows[s:s + 1, :], shape) for s in range(SUB)]
        inside = jnp.logical_and(lane >= base, lane < base + SUB)
        for h in range(g + 1, len(groups)):
            old = groups[h]
            terms = [
                jnp.broadcast_to(old[:, base + s:base + s + 1], shape) * reduced[s] for s in range(SUB)
            ]
            while len(terms) > 1:
                terms = [terms[i] + terms[i + 1] for i in range(0, len(terms), 2)]
            groups[h] = jnp.where(inside, 0.0, old) - terms[0]
    return jnp.concatenate(groups, axis=0)


def factor_kernel(a_ref, l_ref, x_ref, w_ref):
    size = a_ref.shape[0]
    count = size // BLK
    row_id = lax.broadcasted_iota(jnp.int32, (BLK, BLK), 0)
    col_id = lax.broadcasted_iota(jnp.int32, (BLK, BLK), 1)

    @pl.loop(0, count)
    def _(i):
        at = pl.ds(pl.multiple_of(i * BLK, BLK), BLK)
        w_ref[at, :] = a_ref[at, :]
        l_ref[at, :] = jnp.zeros((BLK, size), F32)

    @pl.loop(0, count)
    def _(k):
        at = pl.ds(pl.multiple_of(k * BLK, BLK), BLK)
        done = eliminate(w_ref[at, at])
        pivots = jnp.sum(jnp.where(row_id == col_id, done, 0.0), axis=1, keepdims=True)
        scale = 1.0 / jnp.sqrt(pivots)
        upper = jnp.where(col_id >= row_id, done * scale, 0.0)
        inner = jnp.where(col_id < row_id, done * scale, 0.0) + jnp.where(row_id == col_id, scale, 0.0)
        l_ref[at, at] = upper.T
        row = dot(inner, w_ref[at, :])
        block_id = lax.broadcasted_iota(jnp.int32, (BLK, size), 1) // BLK
        row = jnp.where(block_id == k, jnp.concatenate([inner] * count, axis=1), row)
        x_ref[at, :] = jnp.where(block_id <= k, row, 0.0)
        inner_t = inner.T

        @pl.loop(k + 1, count)
        def _(i):
            there = pl.ds(pl.multiple_of(i * BLK, BLK), BLK)
            left = dot(w_ref[there, at], inner_t)
            l_ref[there, at] = left
            w_ref[there, at] = jnp.zeros((BLK, BLK), F32)
            w_ref[there, :] = w_ref[there, :] - dot(left, row)


def factor(a):
    size = a.shape[0]
    shape = jax.ShapeDtypeStruct((size, size), F32)
    return pl.pallas_call(
        factor_kernel,
        out_shape=(shape, shape),
        in_specs=[pl.BlockSpec(memory_space=pltpu.VMEM)],
        out_specs=(pl.BlockSpec(memory_space=pltpu.VMEM),) * 2,
        scratch_shapes=[pltpu.VMEM((size, size), F32)],
        compiler_params=pltpu.CompilerParams(vmem_limit_bytes=32 * 1024 * 1024),
        cost_estimate=pl.CostEstimate(flops=60_000_000_000, bytes_accessed=3 * size * size * 4, transcendentals=0),
        name="factor",
    )(a)


def left_kernel(v_ref, pivot_ref, u_ref, out_ref):
    inner = lax.dot_general(
        v_ref[...], pivot_ref[...], (((0,), (0,)), ((), ())), preferred_element_type=F32
    ).astype(jnp.bfloat16)
    out_ref[...] = jnp.dot(u_ref[...], inner, preferred_element_type=F32).astype(jnp.bfloat16)


def left_factors(v, pivot_v, u):
    slots = v.shape[0] // TILE
    rows = u.shape[0] // slots
    return pl.pallas_call(
        left_kernel,
        grid=(v.shape[1] // RANK, slots),
        out_shape=jax.ShapeDtypeStruct(u.shape, jnp.bfloat16),
        in_specs=[
            pl.BlockSpec((TILE, RANK), lambda j, t: (t, j)),
            pl.BlockSpec((TILE, RANK), lambda j, t: (0, j)),
            pl.BlockSpec((rows, RANK), lambda j, t: (t, j)),
        ],
        out_specs=pl.BlockSpec((rows, RANK), lambda j, t: (t, j)),
        cost_estimate=pl.CostEstimate(
            flops=2 * v.size * RANK + 2 * u.size * RANK,
            bytes_accessed=2 * (v.size + 2 * u.size + pivot_v.size),
            transcendentals=0,
        ),
        name="left",
    )(v, pivot_v, u)


def place(block, width, start):
    return lax.dynamic_update_slice_in_dim(jnp.zeros((block.shape[0], width), block.dtype), block, start, 1)


def local(mesh, panel_tiles, left_u, earlier_right_factors, tile_global_index):
    row_devices = mesh.shape["row"]
    tile_count = tile_global_index.shape[0]
    rows, col_width = panel_tiles.shape
    slots = rows // TILE
    pivot_position = jnp.sum(
        jnp.where(tile_global_index == 0, jnp.arange(tile_count, dtype=jnp.int32), 0)
    )
    owner_row = pivot_position // slots
    local_slot = pivot_position % slots
    my_row = lax.axis_index("row")
    my_col = lax.axis_index("col")
    mine = my_row == owner_row

    def owned(value):
        part = lax.dynamic_slice_in_dim(value, local_slot * TILE, TILE, 0)
        return jnp.where(mine, part, jnp.zeros_like(part))

    pivot_right, pivot_left = lax.psum((owned(earlier_right_factors), owned(left_u)), "row")
    pivot_panel = lax.psum_scatter(owned(panel_tiles), "row", scatter_dimension=0, tiled=True)

    share = TILE // row_devices
    my_left = lax.dynamic_slice_in_dim(pivot_left, my_row * share, share, 0)
    pivot_small = left_factors(pivot_right, pivot_right, my_left)
    contract = (((1,), (1,)), ((), ()))
    pivot_terms = lax.dot_general(pivot_small, pivot_left, contract, preferred_element_type=F32)
    diagonal = lax.psum_scatter(
        place(pivot_panel, TILE, my_col * col_width) - pivot_terms, "col", scatter_dimension=0, tiled=True
    )
    diagonal = lax.all_gather(diagonal, ("row", "col"), axis=0, tiled=True)

    left_small = left_factors(earlier_right_factors, pivot_right, left_u)
    update_terms = lax.dot_general(left_small, pivot_left, contract, preferred_element_type=F32)
    partial = place(panel_tiles, TILE, my_col * col_width) - update_terms
    updated = lax.psum_scatter(partial, "col", scatter_dimension=0, tiled=True)

    chol, inverse = factor((diagonal + diagonal.T) * 0.5)
    solved = lax.dot_general(updated, inverse, contract, precision=HI, preferred_element_type=F32)
    held = updated.shape[0]
    first = my_col * held
    chosen = jnp.logical_and(mine, first // TILE == local_slot)
    chol_rows = lax.dynamic_slice_in_dim(chol, first % TILE, held, 0)
    solved = jnp.where(chosen, chol_rows, solved)
    return lax.all_to_all(solved, "col", split_axis=1, concat_axis=0, tiled=True)


def solution(mesh):
    in_specs = (P("row", "col"), P("row", "col"), P("row", "col"), P())
    return jax.shard_map(
        functools.partial(local, mesh), mesh=mesh, in_specs=in_specs, out_specs=P("row", "col"), check_vma=False
    )
```

time: 912 us -> 472 us (0.52); the launches traced: 901 us -> 471 us
  other arithmetic: 270 us -> 15.4 us
  waiting for transfers between devices: 416 us -> 251 us
  Pallas kernels: 0 us -> 89.2 us
  local copies, waits for them, and re-layouts: 103 us -> 20.8 us
  matrix products: 90.7 us -> 26.4 us
  blocking collectives: 0 us -> 52.2 us
    psum x3 -> x1, waiting for transfers between devices: 416 us -> 105 us  [local(): lax.psum((owned(earlier_right_factors), owned(left_u)), 'row')]
    another operation x34 -> x0, other arithmetic: 256 us -> none  [the longest x31 173 us: local(): cholesky_factor = jnp.linalg.cholesky(diagonal)]
    reduce_scatter x0 -> x3, waiting for transfers between devices: none -> 119 us  [the longest x1 64.8 us: local(): updated = lax.psum_scatter(partial, 'col', scatter_dimension=0, tiled=True)]
    pallas_call x0 -> x3, Pallas kernels: none -> 89.2 us  [the longest x1 66.3 us: factor(): pl.pallas_call(factor_kernel, out_shape=(shape, shape), in_specs=[pl.Bloc...]
    all_to_all x0 -> x1, blocking collectives: none -> 52.2 us  [local(): lax.all_to_all(solved, 'col', split_axis=1, concat_axis=0, tiled=True)]
    another operation x29 -> x0, matrix products: 45.3 us -> none  [the longest x14 23.1 us: local(): cholesky_factor = jnp.linalg.cholesky(diagonal)]
    all_gather x0 -> x1, waiting for transfers between devices: none -> 27.4 us  [local(): diagonal = lax.all_gather(diagonal, ('row', 'col'), axis=0, tiled=True)]
    reshape x2 -> x0, local copies, waits for them, and re-layouts: 27 us -> none  [the longest x1 13.5 us: local(): left_blocks = left_u.reshape(TILE_DEV, TILE, COL_DEV, RANK)]
  transfers between devices with their start and end apart: 3 -> 5, of which waited for: 3 -> 5; matrix products, arithmetic and copies ran while one was open for 4% -> 8% of each run, Pallas kernels for 0% -> 17%
where the time goes in v1:
time: 472 us; the launch traced here: 471 us
  waiting for transfers between devices  251 us (53%)
  Pallas kernels  89.2 us (19%)
  blocking collectives  52.2 us (11%)
  matrix products  26.4 us (6%)
  local copies, waits for them, and re-layouts  20.8 us (4%)
  between operations  15.9 us (3%)
  other arithmetic  15.4 us (3%)
    psum x1, waiting for transfers between devices, local(): lax.psum((owned(earlier_right_factors), owned(left_u)), 'row')  105 us
    pallas_call x1, Pallas kernels, factor(): pl.pallas_call(factor_kernel, out_shape=(shape, shape), in_specs=[pl.Bloc...  66.3 us
    reduce_scatter x1, waiting for transfers between devices, local(): updated = lax.psum_scatter(partial, 'col', scatter_dimension=0, tiled=True)  64.8 us
    all_to_all x1, blocking collectives, local(): lax.all_to_all(solved, 'col', split_axis=1, concat_axis=0, tiled=True)  52.2 us
    reduce_scatter x1, waiting for transfers between devices, local(): lax.psum_scatter(owned(panel_tiles), 'row', scatter_dimension=0, tiled=True)  32.1 us
    all_gather x1, waiting for transfers between devices, local(): diagonal = lax.all_gather(diagonal, ('row', 'col'), axis=0, tiled=True)  27.4 us
    pallas_call x2, Pallas kernels, left_factors(): pl.pallas_call(left_kernel, grid=(v.shape[1] // RANK, slots), out_shape=j...  22.9 us
    reduce_scatter x1, waiting for transfers between devices, local(): lax.psum_scatter(place(pivot_panel, TILE, my_col * col_width) - pivot_ter...  22.1 us
  transfers between devices with their start and end apart: 5, of which 5 were waited for; matrix products, arithmetic and copies ran while one was open for 8% of the time, Pallas kernels for 17%

profile of v1, /device:TPU:0, one launch (start us, length us, event | category | flops | bytes accessed | tf_op | source)
XLA Modules:
  0.0 471.5 jit_solution(5773188793346719554)
XLA Ops:
  6.5 0.0 reduce-scatter.6.cloned.1.call-start
  6.5 1.3 fusion.1
  10.5 2.3 dynamic-slice_select_fusion.3
  12.7 0.0 reduce-scatter.6.cloned.1.call-update
  12.7 0.0 all-reduce.3.cloned.1.call-start
  12.8 6.6 %dynamic-slice_select_fusion = (bf16[1024,1536]{1,0:T(8,128)(2,1)}, bf16[1024,1536]{1,0:T(8,128)(2,1)}) fusion(bf16[2048,1536]{1,0:T(8,128)(2,1)} %u_ref.1, s32[]{:T(128)S(6)} %select_n.71, pred[]{:T(512)S(6)} %eq.13, bf16[2048,1536]{1,0:T(8,128)(2,1)} %v_ref.1), kind=kLoop, calls=%fused_computation.3 | loop fusion | flops 3145728 | bytes 12582917 | tf_op jit(solution)/shard_map/jit(_where)/select_n | solution.py:162
  19.4 0.0 all-reduce.3.cloned.1.call-update
  19.4 0.0 reduce-scatter.10.cloned.1.call-start
  19.5 32.1 %reduce-scatter.6.cloned.1.call-done = f32[128,256]{1,0:T(8,128)} async-done(((f32[1024,256]{1,0:T(8,128)}), f32[128,256]{1,0:T(8,128)}) %reduce-scatter.6.cloned.1.call-update) | async-done | bytes 131088 | tf_op jit(solution)/shard_map/reduce_scatter | solution.py:165
  51.6 0.8 broadcast_in_dim.11
  52.4 1.6 constant_dynamic-update-slice_fusion.1
  54.0 104.9 %all-reduce.3.cloned.1.call-done = (bf16[1024,1536]{1,0:T(8,128)(2,1)}, bf16[1024,1536]{1,0:T(8,128)(2,1)}) async-done(((bf16[1024,1536]{1,0:T(8,128)(2,1)}, bf16[1024,1536]{1,0:T(8,128)(2,1)}), (bf16[1024,1536]{1,0:T(8,128)(2,1)}, bf16[1024,1536]{1,0:T(8,128)(2,1)})) %all-reduce.3.cloned.1.call-update) | async-done | bytes 6291472 | tf_op jit(solution)/shard_map/psum | solution.py:164
  158.8 1.8 constant_dynamic-slice_fusion.u_ref
  160.6 0.0 copy-start.3
  160.6 6.8 %left.2 = bf16[128,1536]{1,0:T(8,128)(2,1)} custom-call(bf16[1024,1536]{1,0:T(8,128)(2,1)} %get-tuple-element.9.v_ref.pivot_ref, bf16[1024,1536]{1,0:T(8,128)(2,1)} %get-tuple-element.9.v_ref.pivot_ref, bf16[128,1536]{1,0:T(8,128)(2,1)} %constant_dynamic-slice_fusion.u_ref), custom_call_target="tpu_custom_call" | custom-call | flops 905969664 | bytes 7077888 | tf_op jit(solution)/shard_map/left/pallas_call | solution.py:123
  167.4 0.0 copy-done.3
  167.4 3.1 convolution_subtract_fusion.1
  170.5 0.0 reduce-scatter.10.cloned.1.call-update
  170.5 0.0 all-gather.2.cloned.1.call-start
  170.6 22.1 %reduce-scatter.10.cloned.1.call-done = f32[32,1024]{1,0:T(8,128)} async-done(((f32[128,1024]{1,0:T(8,128)}), f32[32,1024]{1,0:T(8,128)}) %reduce-scatter.10.cloned.1.call-update) | async-done | bytes 131088 | tf_op jit(solution)/shard_map/reduce_scatter | solution.py:172
  192.6 0.0 all-gather.2.cloned.1.call-update
  192.7 0.0 copy-start.2
  192.7 0.2 reduce-scatter.8.cloned.1.call-start
  192.9 4.3 broadcast_in_dim.13
  197.2 0.0 copy-done.2
  197.2 1.5 constant_dynamic-update-slice_fusion
  198.7 0.0 copy-start.4
  198.7 16.1 %left.3 = bf16[2048,1536]{1,0:T(8,128)(2,1)} custom-call(bf16[2048,1536]{1,0:T(8,128)(2,1)} %v_ref.1, bf16[1024,1536]{1,0:T(8,128)(2,1)} %get-tuple-element.9.v_ref.pivot_ref, bf16[2048,1536]{1,0:T(8,128)(2,1)} %u_ref.1), custom_call_target="tpu_custom_call" | custom-call | flops 3221225472 | bytes 22020096 | tf_op jit(solution)/shard_map/left/pallas_call | solution.py:123
  214.8 0.0 copy-done.4
  214.8 13.1 %convolution_subtract_fusion = f32[2048,1024]{1,0:T(8,128)} fusion(f32[2048,1024]{1,0:T(8,128)} %constant_dynamic-update-slice_fusion, bf16[2048,1536]{1,0:T(8,128)(2,1)} %left.3, bf16[1024,1536]{1,0:T(8,128)(2,1)S(1)} %copy-done.4), kind=kOutput, calls=%fused_computation.2 | convolution fusion | flops 6444548096 | bytes 26214400 | tf_op jit(solution)/shard_map/dot_general | solution.py:178
  228.0 0.0 reduce-scatter.8.cloned.1.call-update
  228.0 27.4 %all-gather.2.cloned.1.call-done = f32[1024,1024]{1,0:T(8,128)} async-done(((f32[32,1024]{1,0:T(8,128)}), f32[1024,1024]{1,0:T(8,128)}) %all-gather.2.cloned.1.call-update) | async-done | bytes 4194320 | tf_op jit(solution)/shard_map/all_gather | solution.py:175
  255.4 5.4 %copy.11 = f32[1024,1024]{0,1:T(8,128)} copy(f32[1024,1024]{1,0:T(8,128)} %all-gather.2.cloned.1.call-done) | data formatting | bytes 8388608 | tf_op jit(solution)/shard_map/all_gather | solution.py:175
  260.8 5.2 %fusion.a_ref = f32[1024,1024]{1,0:T(8,128)S(1)} fusion(f32[1024,1024]{1,0:T(8,128)} %all-gather.2.cloned.1.call-done, f32[1024,1024]{0,1:T(8,128)} %copy.11), kind=kLoop, calls=%fused_computation.1 | loop fusion | flops 2097152 | bytes 12582912 | tf_op jit(solution)/shard_map/mul | solution.py:182
  266.0 66.3 %factor.1 = (f32[1024,1024]{1,0:T(8,128)S(1)}, f32[1024,1024]{1,0:T(8,128)S(1)}) custom-call(f32[1024,1024]{1,0:T(8,128)S(1)} %fusion.a_ref), custom_call_target="tpu_custom_call" | custom-call | flops 60000002048 | bytes 12582912 | tf_op jit(solution)/shard_map/factor/pallas_call | solution.py:101
  332.3 0.0 copy-start
  332.3 1.9 copy-done
  334.2 0.0 copy-start.1
  334.2 2.0 copy-done.1
  336.2 64.8 %reduce-scatter.8.cloned.1.call-done = f32[512,1024]{1,0:T(8,128)} async-done(((f32[2048,1024]{1,0:T(8,128)}), f32[512,1024]{1,0:T(8,128)}) %reduce-scatter.8.cloned.1.call-update) | async-done | bytes 2097168 | tf_op jit(solution)/shard_map/reduce_scatter | solution.py:180
  401.0 10.2 %dynamic-slice_select_fusion.2 = f32[512,1024]{1,0:T(8,128)S(1)} fusion(f32[1024,1024]{1,0:T(8,128)} %copy-done.1, s32[]{:T(128)S(6)} %select_n.79, f32[512,1024]{1,0:T(8,128)} %reduce-scatter.8.cloned.1.call-done, f32[1024,1024]{1,0:T(8,128)} %copy-done, pred[]{:T(512)S(6)} %and.26), kind=kOutput, calls=%fused_computation.6 | convolution fusion | flops 6442975232 | bytes 10485765 | tf_op jit(solution)/shard_map/dot_general | solution.py:183
  411.2 0.2 copy.17
  411.4 52.2 %all_to_all.19 = f32[512,4,256]{2,0,1:T(8,128)S(1)} all-to-all(f32[512,4,256]{2,0,1:T(8,128)S(1)} %bitcast.18), channel_id=1, replica_groups=mesh['row'=8,'col'=4] {'col'}, dimensions={1} | all-to-all | bytes 4194304 | tf_op jit(solution)/shard_map/all_to_all | solution.py:189
  463.6 1.3 copy.23
Async XLA Ops:
  6.5 45.0 %reduce-scatter.6.cloned.1.call-start = ((), (), s32[]{:S(2)}) async-start(), calls=%async_computation.4 | async-start | bytes 1179648 | tf_op jit(solution)/shard_map/reduce_scatter | solution.py:165
  12.7 146.1 %all-reduce.3.cloned.1.call-start = ((), (), s32[]{:S(2)}) async-start(), calls=%async_computation.8 | async-start | bytes 12582912 | tf_op jit(solution)/shard_map/psum | solution.py:164
  19.4 173.2 %reduce-scatter.10.cloned.1.call-start = ((), (), s32[]{:S(2)}) async-start(), calls=%async_computation.7 | async-start | bytes 655360 | tf_op jit(solution)/shard_map/reduce_scatter | solution.py:172
  160.6 6.8 %copy-start.3 = (bf16[1024,1536]{1,0:T(8,128)(2,1)S(1)}, bf16[1024,1536]{1,0:T(8,128)(2,1)}, u32[]{:S(2)}) copy-start(bf16[1024,1536]{1,0:T(8,128)(2,1)} %get-tuple-element.10) | copy-start | bytes 9437188
  170.5 84.9 %all-gather.2.cloned.1.call-start = ((), (), s32[]{:S(2)}) async-start(), calls=%async_computation.5 | async-start | bytes 4325376 | tf_op jit(solution)/shard_map/all_gather | solution.py:175
  192.7 4.5 copy-start.2
  192.7 208.4 %reduce-scatter.8.cloned.1.call-start = ((), (), s32[]{:S(2)}) async-start(), calls=%async_computation.6 | async-start | bytes 10485760 | tf_op jit(solution)/shard_map/reduce_scatter | solution.py:180
  198.7 16.1 %copy-start.4 = (bf16[1024,1536]{1,0:T(8,128)(2,1)S(1)}, bf16[1024,1536]{1,0:T(8,128)(2,1)}, u32[]{:S(2)}) copy-start(bf16[1024,1536]{1,0:T(8,128)(2,1)} %get-tuple-element.10) | copy-start | bytes 9437188
  332.3 1.9 copy-start
  334.2 2.0 copy-start.1
Sparse Core Ops, SparseCore 0:
  12.9 38.6 reduce-scatter.5
  54.9 103.9 all-reduce.2
  170.6 21.9 reduce-scatter.9
  195.5 59.8 all-gather.1
  257.6 143.3 reduce-scatter.7

commit v2 on v1

--- a/solution.py
+++ b/solution.py
@@ -139,6 +139,98 @@
     )(v, pivot_v, u)
 
 
+MESH = pl.DeviceIdType.MESH
+
+
+def exchange_kernel(depth, chips, part_ref, out_ref, got, sends, recvs, pair_send, pair_recv):
+    me = lax.axis_index("row")
+    col = lax.axis_index("col")
+    chip, core = me // 2, me % 2
+    share = part_ref.shape[0]
+    sub = share // depth
+    pair = chip * 2 + 1 - core
+    cols = [(col + d) % depth for d in range(1, depth)]
+    peers = [((chip + d) % chips) * 2 + core for d in range(1, chips)]
+
+    barrier = pltpu.get_barrier_semaphore()
+    for other in cols:
+        pl.semaphore_signal(barrier, inc=1, device_id=(me, other), device_id_type=MESH)
+    for other in peers + [pair]:
+        pl.semaphore_signal(barrier, inc=1, device_id=(other, col), device_id_type=MESH)
+    pl.semaphore_wait(barrier, depth + chips - 1)
+
+    def copy(src, dst, i, target):
+        return pltpu.make_async_remote_copy(
+            src_ref=src, dst_ref=dst, send_sem=sends.at[i], recv_sem=recvs.at[i],
+            device_id=target, device_id_type=MESH,
+        )
+
+    first = []
+    for d, other in enumerate(cols):
+        rows = pl.ds(pl.multiple_of(other * sub, sub), sub)
+        first.append(copy(part_ref.at[rows, :], got.at[d], d, (me, other)))
+        first[-1].start()
+    total = part_ref[pl.ds(pl.multiple_of(col * sub, sub), sub), :]
+    for d, item in enumerate(first):
+        item.wait_recv()
+        total = total + got[d]
+    mine = pl.ds(pl.multiple_of(me * share + col * sub, sub), sub)
+    out_ref[mine, :] = total
+
+    second = []
+    for d, other in enumerate(cols):
+        second.append(copy(out_ref.at[mine, :], out_ref.at[mine, :], depth - 1 + d, (me, other)))
+        second[-1].start()
+    for item in second:
+        item.wait_recv()
+
+    block = out_ref.at[pl.ds(pl.multiple_of(me * share, share), share), :]
+    third = []
+    for d, other in enumerate(peers):
+        third.append(copy(block, block, 2 * (depth - 1) + d, (other, col)))
+        third[-1].start()
+    fourth = []
+    for d in range(chips):
+        if d:
+            third[d - 1].wait_recv()
+        owner = ((chip + chips - d) % chips) * 2 + core
+        held = out_ref.at[pl.ds(pl.multiple_of(owner * share, share), share), :]
+        fourth.append(
+            pltpu.make_async_remote_copy(
+                src_ref=held, dst_ref=held, send_sem=pair_send.at[d], recv_sem=pair_recv.at[d],
+                device_id=(pair, col), device_id_type=MESH,
+            )
+        )
+        fourth[-1].start()
+    for item in fourth:
+        item.wait_recv()
+    for item in first + second + third + fourth:
+        item.wait_send()
+
+
+def exchange(mesh, part):
+    row_devices, depth = mesh.shape["row"], mesh.shape["col"]
+    chips = row_devices // 2
+    share, width = part.shape
+    links = 2 * (depth - 1) + chips - 1
+    return pl.pallas_call(
+        functools.partial(exchange_kernel, depth, chips),
+        out_shape=jax.ShapeDtypeStruct((share * row_devices, width), F32),
+        in_specs=[pl.BlockSpec(memory_space=pltpu.VMEM)],
+        out_specs=pl.BlockSpec(memory_space=pltpu.VMEM),
+        scratch_shapes=[
+            pltpu.VMEM((depth - 1, share // depth, width), F32),
+            pltpu.SemaphoreType.DMA((links,)),
+            pltpu.SemaphoreType.DMA((links,)),
+            pltpu.SemaphoreType.DMA((chips,)),
+            pltpu.SemaphoreType.DMA((chips,)),
+        ],
+        compiler_params=pltpu.CompilerParams(collective_id=0, has_side_effects=True),
+        cost_estimate=pl.CostEstimate(flops=40_000_000_000, bytes_accessed=share * row_devices * width * 8, transcendentals=0),
+        name="exchange",
+    )(part)
+
+
 def place(block, width, start):
     return lax.dynamic_update_slice_in_dim(jnp.zeros((block.shape[0], width), block.dtype), block, start, 1)
 
@@ -162,21 +254,23 @@
         return jnp.where(mine, part, jnp.zeros_like(part))
 
     pivot_right, pivot_left = lax.psum((owned(earlier_right_factors), owned(left_u)), "row")
-    pivot_panel = lax.psum_scatter(owned(panel_tiles), "row", scatter_dimension=0, tiled=True)
+    pivot_panel, pivot_right, pivot_left = lax.optimization_barrier(
+        (owned(panel_tiles), pivot_right, pivot_left)
+    )
+    pivot_panel = lax.psum_scatter(pivot_panel, "row", scatter_dimension=0, tiled=True)
 
     share = TILE // row_devices
     my_left = lax.dynamic_slice_in_dim(pivot_left, my_row * share, share, 0)
     pivot_small = left_factors(pivot_right, pivot_right, my_left)
     contract = (((1,), (1,)), ((), ()))
     pivot_terms = lax.dot_general(pivot_small, pivot_left, contract, preferred_element_type=F32)
-    diagonal = lax.psum_scatter(
-        place(pivot_panel, TILE, my_col * col_width) - pivot_terms, "col", scatter_dimension=0, tiled=True
-    )
-    diagonal = lax.all_gather(diagonal, ("row", "col"), axis=0, tiled=True)
+    diagonal = place(pivot_panel, TILE, my_col * col_width) - pivot_terms
 
     left_small = left_factors(earlier_right_factors, pivot_right, left_u)
     update_terms = lax.dot_general(left_small, pivot_left, contract, preferred_element_type=F32)
     partial = place(panel_tiles, TILE, my_col * col_width) - update_terms
+    partial, diagonal = lax.optimization_barrier((partial, diagonal))
+    diagonal = exchange(mesh, diagonal)
     updated = lax.psum_scatter(partial, "col", scatter_dimension=0, tiled=True)
 
     chol, inverse = factor((diagonal + diagonal.T) * 0.5)

time: 472 us -> 400 us (0.85)
  waiting for transfers between devices: 251 us -> 110 us
  Pallas kernels: 89.2 us -> 157 us
    pallas_call x0 -> x1, Pallas kernels: none -> 68.2 us  [exchange(): pl.pallas_call(functools.partial(exchange_kernel, depth, chips), out_shap...]
    reduce_scatter x1, waiting for transfers between devices: 64.8 us -> 9.79 us  [local(): updated = lax.psum_scatter(partial, 'col', scatter_dimension=0, tiled=True)]
    reduce_scatter x2 -> x1, waiting for transfers between devices: 54.2 us -> 2.17 us  [local(): lax.psum_scatter(pivot_panel, 'row', scatter_dimension=0, tiled=True)]
    all_gather x1 -> x0, waiting for transfers between devices: 27.4 us -> none  [local(): diagonal = lax.all_gather(diagonal, ('row', 'col'), axis=0, tiled=True)]
    psum x1, waiting for transfers between devices: 105 us -> 98.4 us  [local(): lax.psum((owned(earlier_right_factors), owned(left_u)), 'row')]
    all_gather x1 -> x0, local copies, waits for them, and re-layouts: 5.38 us -> none  [local(): diagonal = lax.all_gather(diagonal, ('row', 'col'), axis=0, tiled=True)]
    pallas_call x0 -> x1, local copies, waits for them, and re-layouts: none -> 5.36 us  [exchange(): pl.pallas_call(functools.partial(exchange_kernel, depth, chips), out_shap...]
  transfers between devices with their start and end apart: 5 -> 3, of which waited for: 5 -> 3; matrix products, arithmetic and copies ran while one was open for 8% -> 8% of each run, Pallas kernels for 17% -> 39%
where the time goes in v2:
time: 400 us; the launch traced here: 399 us
  Pallas kernels  157 us (39%)
  waiting for transfers between devices  110 us (28%)
  blocking collectives  56.6 us (14%)
  matrix products  25.2 us (6%)
  local copies, waits for them, and re-layouts  19.8 us (5%)
  between operations  15.9 us (4%)
  other arithmetic  13.4 us (3%)
    psum x1, waiting for transfers between devices, local(): lax.psum((owned(earlier_right_factors), owned(left_u)), 'row')  98.4 us
    pallas_call x1, Pallas kernels, exchange(): pl.pallas_call(functools.partial(exchange_kernel, depth, chips), out_shap...  68.2 us
    pallas_call x1, Pallas kernels, factor(): pl.pallas_call(factor_kernel, out_shape=(shape, shape), in_specs=[pl.Bloc...  66.3 us
    all_to_all x1, blocking collectives, local(): lax.all_to_all(solved, 'col', split_axis=1, concat_axis=0, tiled=True)  56.6 us
    pallas_call x2, Pallas kernels, left_factors(): pl.pallas_call(left_kernel, grid=(v.shape[1] // RANK, slots), out_shape=j...  23 us
    dot_general x1, matrix products, local(): lax.dot_general(left_small, pivot_left, contract, preferred_element_type=...  13.1 us
    dot_general x1, matrix products, local(): lax.dot_general(updated, inverse, contract, precision=HI, preferred_eleme...  10.2 us
    reduce_scatter x1, waiting for transfers between devices, local(): updated = lax.psum_scatter(partial, 'col', scatter_dimension=0, tiled=True)  9.79 us
  transfers between devices with their start and end apart: 3, of which 3 were waited for; matrix products, arithmetic and copies ran while one was open for 8% of the time, Pallas kernels for 39%

profile of v2, /device:TPU:0, one launch (start us, length us, event | category | flops | bytes accessed | tf_op | source)
XLA Modules:
  0.0 399.1 jit_solution(16860915745136597625)
XLA Ops:
  6.5 0.0 all-reduce.3.cloned.1.call-start
  6.5 1.3 fusion.1
  10.5 6.6 %dynamic-slice_select_fusion = (bf16[1024,1536]{1,0:T(8,128)(2,1)}, bf16[1024,1536]{1,0:T(8,128)(2,1)}) fusion(bf16[2048,1536]{1,0:T(8,128)(2,1)} %u_ref.1, s32[]{:T(128)S(6)} %select_n.72, pred[]{:T(512)S(6)} %eq.13, bf16[2048,1536]{1,0:T(8,128)(2,1)} %v_ref.1), kind=kLoop, calls=%fused_computation.3 | loop fusion | flops 3145728 | bytes 12582917 | tf_op jit(solution)/shard_map/jit(_where)/select_n | solution.py:254
  17.1 0.0 copy-start.2
  17.1 0.0 all-reduce.3.cloned.1.call-update
  17.1 0.0 reduce-scatter.3.cloned.1.call-start
  17.1 1.5 copy-done.2
  18.6 1.0 dynamic-slice_select_fusion.3
  19.7 4.3 %broadcast_in_dim.11 = f32[2048,1024]{1,0:T(8,128)} broadcast(f32[]{:T(128)} %constant.63.clone.1), dimensions={} | broadcast | bytes 8388612 | tf_op jit(solution)/shard_map/broadcast_in_dim | solution.py:235
  24.0 1.5 constant_dynamic-update-slice_fusion.1
  25.5 98.4 %all-reduce.3.cloned.1.call-done = (bf16[1024,1536]{1,0:T(8,128)(2,1)}, bf16[1024,1536]{1,0:T(8,128)(2,1)}) async-done(((bf16[1024,1536]{1,0:T(8,128)(2,1)}, bf16[1024,1536]{1,0:T(8,128)(2,1)}), (bf16[1024,1536]{1,0:T(8,128)(2,1)}, bf16[1024,1536]{1,0:T(8,128)(2,1)})) %all-reduce.3.cloned.1.call-update) | async-done | bytes 6291472 | tf_op jit(solution)/shard_map/psum | solution.py:256
  123.9 0.0 reduce-scatter.3.cloned.1.call-update
  123.9 0.0 copy-start.3
  123.9 0.2 reduce-scatter.5.cloned.1.call-start
  124.2 16.3 %left.2 = bf16[2048,1536]{1,0:T(8,128)(2,1)} custom-call(bf16[2048,1536]{1,0:T(8,128)(2,1)} %v_ref.1, bf16[1024,1536]{1,0:T(8,128)(2,1)} %get-tuple-element.12.pivot_ref.v_ref, bf16[2048,1536]{1,0:T(8,128)(2,1)} %u_ref.1), custom_call_target="tpu_custom_call" | custom-call | flops 3221225472 | bytes 22020096 | tf_op jit(solution)/shard_map/left/pallas_call | solution.py:123
  140.4 0.0 copy-done.3
  140.4 0.8 constant_dynamic-slice_fusion.u_ref
  141.2 6.7 %left.3 = bf16[128,1536]{1,0:T(8,128)(2,1)} custom-call(bf16[1024,1536]{1,0:T(8,128)(2,1)} %get-tuple-element.12.pivot_ref.v_ref, bf16[1024,1536]{1,0:T(8,128)(2,1)} %get-tuple-element.12.pivot_ref.v_ref, bf16[128,1536]{1,0:T(8,128)(2,1)} %constant_dynamic-slice_fusion.u_ref), custom_call_target="tpu_custom_call" | custom-call | flops 905969664 | bytes 7077888 | tf_op jit(solution)/shard_map/left/pallas_call | solution.py:123
  147.9 0.0 copy-start.4
  147.9 13.1 %convolution_subtract_fusion = f32[2048,1024]{1,0:T(8,128)} fusion(f32[2048,1024]{1,0:T(8,128)} %constant_dynamic-update-slice_fusion.1, bf16[2048,1536]{1,0:T(8,128)(2,1)} %left.2, bf16[1024,1536]{1,0:T(8,128)(2,1)S(1)} %copy-done.3), kind=kOutput, calls=%fused_computation.2 | convolution fusion | flops 6444548096 | bytes 26214400 | tf_op jit(solution)/shard_map/dot_general | solution.py:270
  161.0 2.2 reduce-scatter.3.cloned.1.call-done
  163.2 0.9 constant_dynamic-update-slice_fusion
  164.2 0.0 copy-done.4
  164.2 1.9 convolution_subtract_fusion.1.part_ref
  166.1 0.0 reduce-scatter.5.cloned.1.call-update
  166.2 68.2 %exchange.1 = f32[1024,1024]{1,0:T(8,128)} custom-call(f32[128,1024]{1,0:T(8,128)} %convolution_subtract_fusion.1.part_ref), custom_call_target="tpu_custom_call" | custom-call | flops 40000000000 | bytes 8388608 | tf_op jit(solution)/shard_map/exchange/pallas_call | solution.py:216
  234.4 5.4 %copy.7 = f32[1024,1024]{0,1:T(8,128)} copy(f32[1024,1024]{1,0:T(8,128)} %exchange.1) | data formatting | bytes 8388608 | tf_op jit(solution)/shard_map/exchange/pallas_call | solution.py:216
  239.7 4.5 %fusion.a_ref = f32[1024,1024]{1,0:T(8,128)S(1)} fusion(f32[1024,1024]{1,0:T(8,128)} %exchange.1, f32[1024,1024]{0,1:T(8,128)} %copy.7), kind=kLoop, calls=%fused_computation.1 | loop fusion | flops 2097152 | bytes 12582912 | tf_op jit(solution)/shard_map/mul | solution.py:276
  244.2 66.3 %factor.1 = (f32[1024,1024]{1,0:T(8,128)S(1)}, f32[1024,1024]{1,0:T(8,128)S(1)}) custom-call(f32[1024,1024]{1,0:T(8,128)S(1)} %fusion.a_ref), custom_call_target="tpu_custom_call" | custom-call | flops 60000002048 | bytes 12582912 | tf_op jit(solution)/shard_map/factor/pallas_call | solution.py:101
  310.6 0.0 copy-start
  310.6 1.9 copy-done
  312.5 0.0 copy-start.1
  312.5 2.0 copy-done.1
  314.5 9.8 %reduce-scatter.5.cloned.1.call-done = f32[512,1024]{1,0:T(8,128)} async-done(((f32[2048,1024]{1,0:T(8,128)}), f32[512,1024]{1,0:T(8,128)}) %reduce-scatter.5.cloned.1.call-update) | async-done | bytes 2097168 | tf_op jit(solution)/shard_map/reduce_scatter | solution.py:274
  324.3 10.2 %dynamic-slice_select_fusion.2 = f32[512,1024]{1,0:T(8,128)S(1)} fusion(f32[1024,1024]{1,0:T(8,128)} %copy-done.1, s32[]{:T(128)S(6)} %select_n.79, f32[512,1024]{1,0:T(8,128)} %reduce-scatter.5.cloned.1.call-done, f32[1024,1024]{1,0:T(8,128)} %copy-done, pred[]{:T(512)S(6)} %and.26), kind=kOutput, calls=%fused_computation.6 | convolution fusion | flops 6442975232 | bytes 10485765 | tf_op jit(solution)/shard_map/dot_general | solution.py:277
  334.4 0.2 copy.11
  334.6 56.6 %all_to_all.19 = f32[512,4,256]{2,0,1:T(8,128)S(1)} all-to-all(f32[512,4,256]{2,0,1:T(8,128)S(1)} %bitcast.17), channel_id=1, replica_groups=mesh['row'=8,'col'=4] {'col'}, dimensions={1} | all-to-all | bytes 4194304 | tf_op jit(solution)/shard_map/all_to_all | solution.py:283
  391.2 1.3 copy.17
  (1 shorter events, 0.0 us)
Async XLA Ops:
  6.5 117.4 %all-reduce.3.cloned.1.call-start = ((), (), s32[]{:S(2)}) async-start(), calls=%async_computation.5 | async-start | bytes 12582912 | tf_op jit(solution)/shard_map/psum | solution.py:256
  17.1 1.6 copy-start.2
  17.1 146.1 %reduce-scatter.3.cloned.1.call-start = ((), (), s32[]{:S(2)}) async-start(), calls=%async_computation.3 | async-start | bytes 1179648 | tf_op jit(solution)/shard_map/reduce_scatter | solution.py:260
  123.9 16.5 %copy-start.3 = (bf16[1024,1536]{1,0:T(8,128)(2,1)S(1)}, bf16[1024,1536]{1,0:T(8,128)(2,1)}, u32[]{:S(2)}) copy-start(bf16[1024,1536]{1,0:T(8,128)(2,1)} %get-tuple-element.13) | copy-start | bytes 9437188
  123.9 200.3 %reduce-scatter.5.cloned.1.call-start = ((), (), s32[]{:S(2)}) async-start(), calls=%async_computation.4 | async-start | bytes 10485760 | tf_op jit(solution)/shard_map/reduce_scatter | solution.py:274
  147.9 16.3 %copy-start.4 = (bf16[128,1536]{1,0:T(8,128)(2,1)S(1)}, bf16[128,1536]{1,0:T(8,128)(2,1)}, u32[]{:S(2)}) copy-start(bf16[128,1536]{1,0:T(8,128)(2,1)} %left.3) | copy-start | bytes 1179652
  310.6 1.9 copy-start
  312.5 2.0 copy-start.1
Sparse Core Ops, SparseCore 0:
  17.2 106.6 all-reduce.2
  127.1 36.0 reduce-scatter.2
  166.2 157.9 reduce-scatter.4
